TPU v7x, 512 devices: a whole 4x4x16 slice. The times are simulated.
512 devices in a mesh: sub: 128 (over z_lo, x, y, core), grp: 4 (over z_hi).
Axes of the slice: x: 4, y: 4, z: 16 (z_hi: 4, z_lo: 4; z = z_hi * 4 + z_lo), core: 2. Of those that a mesh axis runs over, the one named last changes fastest.
Arguments:
- load_terms: float32 [128, 4, 512, 384], P('sub', 'grp'), may hold values from -6 to 6
- schur_matrix: float32 [128, 4, 512, 512], P('sub', 'grp'), may hold values from -1 to 4
- local_inverse: float32 [128, 4, 512, 512], P('sub', 'grp'), may hold values from -0.3 to 1
- coarse_modes: float32 [128, 4, 512, 128], P('sub', 'grp'), may hold values from -0.25 to 0.25
- cluster_inverse: float32 [128, 512, 512], P('sub', None, 'grp'), may hold values from -0.5 to 2, as said below
- row_blocks: int32 [128, 4, 4, 96], P('sub', 'grp'), may hold values from 0 to 511, as said below
Outputs:
- solution: float32 [128, 4, 512, 384], P('sub', 'grp')
- residual: float32 [128, 4, 512, 384], P('sub', 'grp')
Inputs may be any that keep to these rules, and one draw needn't show every extreme that they name: `row_blocks`: for each subdomain the four blocks hold 384 different rows. `cluster_inverse`: each cluster's matrix is symmetric.
All inputs are finite; a program needn't handle non-finite values.
Results may differ from a plain program's by a relative error of at most 0.00016.
Values sent between devices are 32-bit elements; how exact they have to be, the bound alone decides.
A program may use at most 64 MiB of HBM per device.

v0:
```python
import jax
import jax.numpy as jnp
from jax import lax
from jax.sharding import PartitionSpec as P

ITERS = 2
ROW_SUBS = 4


relax = 0.5
highest = lax.Precision.HIGHEST


def padded(block, sides, width):
    for axis, dim in sides:
        count = lax.axis_size(axis)
        forward = [(i, i + 1) for i in range(count - 1)]
        backward = [(target, source) for source, target in forward]
        low = lax.ppermute(
            lax.slice_in_dim(block, block.shape[dim] - width, None, axis=dim), axis, forward
        )
        high = lax.ppermute(lax.slice_in_dim(block, 0, width, axis=dim), axis, backward)
        block = jnp.concatenate([low, block, high], axis=dim)
    return block


def from_behind(shard, axis, by):
    count = lax.axis_size(axis)
    pairs = [(i, i + by) for i in range(count) if 0 <= i + by < count]
    return lax.ppermute(shard, axis, pairs)


def matmul(left, right):
    return jnp.dot(left, right, precision=highest, preferred_element_type=jnp.float32)


def local(load_terms, schur_matrix, local_inverse, coarse_modes, cluster_inverse, row_blocks):
    local_load = load_terms[0, 0]
    local_schur = schur_matrix[0, 0]
    local_solve = local_inverse[0, 0]
    mode_basis = coarse_modes[0, 0]
    cluster_cols = cluster_inverse[0]
    block_rows = row_blocks[0, 0]
    block_width = block_rows.shape[1]
    row_total = local_schur.shape[0]
    flat_rows = block_rows.reshape(-1)
    sub_index = lax.axis_index("sub")
    sub_total = lax.axis_size("sub")
    present = jnp.stack(
        [
            sub_index > 0,
            sub_index < sub_total - 1,
            sub_index >= ROW_SUBS,
            sub_index < sub_total - ROW_SUBS,
        ]
    ).astype(jnp.float32)
    halves = jnp.where(present > 0, 0.5, 1.0)
    marks = jnp.broadcast_to(halves[:, None], (4, block_width)).reshape(-1)
    weight = jnp.ones((row_total,), jnp.float32).at[flat_rows].set(marks)[:, None]

    def assemble(vector_rows):
        picked = vector_rows[flat_rows].reshape(4, block_width, -1)
        sideways = jnp.concatenate([picked[0], picked[1]], axis=0)
        extended = padded(sideways, (("sub", 0),), block_width)
        from_left = extended[:block_width]
        from_right = extended[-block_width:]
        from_below = from_behind(picked[3], "sub", ROW_SUBS)
        from_above = from_behind(picked[2], "sub", -ROW_SUBS)
        incoming = (
            jnp.stack([from_left, from_right, from_below, from_above]) * present[:, None, None]
        )
        return vector_rows.at[flat_rows].add(incoming.reshape(4 * block_width, -1))

    residual = assemble(local_load)
    solution = jnp.zeros_like(local_load)
    for iteration in range(ITERS):
        weighted = weight * residual
        fine_part = matmul(local_solve, weighted)
        projected = lax.dot_general(
            mode_basis,
            weighted,
            (((0,), (0,)), ((), ())),
            precision=highest,
            preferred_element_type=jnp.float32,
        )
        partial_terms = matmul(cluster_cols, projected)
        coarse = lax.psum_scatter(partial_terms, "grp", scatter_dimension=0, tiled=True)
        correction = matmul(mode_basis, coarse)
        solution = solution + relax * assemble(weight * (fine_part + correction))
        residual = assemble(local_load - matmul(local_schur, solution))
    return (solution[None, None], residual[None, None])


def solution(mesh):
    return jax.shard_map(
        local,
        mesh=mesh,
        in_specs=(
            P("sub", "grp", None, None),
            P("sub", "grp", None, None),
            P("sub", "grp", None, None),
            P("sub", "grp", None, None),
            P("sub", None, "grp"),
            P("sub", "grp", None, None),
        ),
        out_specs=(P("sub", "grp", None, None), P("sub", "grp", None, None)),
        check_vma=False,
    )
```

profile of v0, /device:TPU:7, one launch (start us, length us, event | category | flops | bytes accessed | tf_op | source)
XLA Modules:
  0.0 286.1 jit_solution(2908115242579123897)
XLA Ops:
  11.0 3.8 %collective-permute-start = (f32[96,384]{1,0:T(8,128)}, f32[96,384]{1,0:T(8,128)S(1)}, u32[]{:S(2)}, u32[]{:S(2)}) collective-permute-start(f32[96,384]{1,0:T(8,128)} %get-tuple-element.22), channel_id=1, source_target_pairs={{0,4},{4,8},{8,12},{12,16},{16,20},{20,24},{24,28},{28,32},{32,36}... | collective-permute-start | bytes 442376 | tf_op jit(solution)/shard_map/ppermute | solution.py:19
  14.8 4.5 %collective-permute-start.2 = (f32[96,384]{1,0:T(8,128)S(1)}, f32[96,384]{1,0:T(8,128)S(1)}, u32[]{:S(2)}, u32[]{:S(2)}) collective-permute-start(f32[96,384]{1,0:T(8,128)S(1)} %get-tuple-element.23), channel_id=1, source_target_pairs={{0,16},{4,20},{8,24},{12,28},{16,32},{20,36},{24,40},{28,44},{32,4... | collective-permute-start | bytes 442376 | tf_op jit(solution)/shard_map/ppermute | solution.py:30
  21.2 3.2 %collective-permute-start.3 = (f32[96,384]{1,0:T(8,128)S(1)}, f32[96,384]{1,0:T(8,128)}, u32[]{:S(2)}, u32[]{:S(2)}) collective-permute-start(f32[96,384]{1,0:T(8,128)S(1)} %get-tuple-element.25), channel_id=1, source_target_pairs={{16,0},{20,4},{24,8},{28,12},{32,16},{36,20},{40,24},{44,28},{48,3... | collective-permute-start | bytes 442376 | tf_op jit(solution)/shard_map/ppermute | solution.py:30
  25.1 2.9 %scatter_custom_fusion = f32[512]{0:T(512)S(1)} fusion(s32[384]{0:T(512)S(1)} %fusion.31, f32[384]{0:T(512)S(1)} %reshape.209, f32[]{:T(128)} %constant.10.clone.1), kind=kCustom, calls=%fused_computation.64 | custom fusion | bytes 2052 | tf_op jit(solution)/shard_map/scatter | solution.py:59
  29.8 3.2 %scatter_fusion = f32[512,384]{1,0:T(8,128)S(1)} fusion(f32[512,384]{1,0:T(8,128)S(1)} %bitcast.88, s32[384]{0:T(512)S(1)} %fusion.31, f32[384,384]{1,0:T(8,128)S(1)} %bitcast_multiply_fusion.4), kind=kCustom, calls=%fused_computation.6 | custom fusion | flops 147456 | bytes 1771008 | tf_op jit(solution)/shard_map/scatter-add | solution.py:72
  36.3 59.8 %reduce-scatter.3.cloned.1.call-done = f32[128,384]{0,1:T(8,128)} async-done(((f32[512,384]{0,1:T(8,128)}), f32[128,384]{0,1:T(8,128)}) %reduce-scatter.3.cloned.1.call-update) | async-done | bytes 196624 | tf_op jit(solution)/shard_map/reduce_scatter | solution.py:87
  97.8 2.7 fusion.1
  102.6 3.8 %collective-permute-start.4 = (f32[96,384]{1,0:T(8,128)S(1)}, f32[96,384]{1,0:T(8,128)S(1)}, u32[]{:S(2)}, u32[]{:S(2)}) collective-permute-start(f32[96,384]{1,0:T(8,128)S(1)} %get-tuple-element.18), channel_id=1, source_target_pairs={{0,4},{4,8},{8,12},{12,16},{16,20},{20,24},{24,28},{28,32},{32,36}... | collective-permute-start | bytes 442376 | tf_op jit(solution)/shard_map/ppermute | solution.py:19
  106.4 4.1 %collective-permute-start.6 = (f32[96,384]{1,0:T(8,128)S(1)}, f32[96,384]{1,0:T(8,128)S(1)}, u32[]{:S(2)}, u32[]{:S(2)}) collective-permute-start(f32[96,384]{1,0:T(8,128)S(1)} %get-tuple-element.19), channel_id=1, source_target_pairs={{0,16},{4,20},{8,24},{12,28},{16,32},{20,36},{24,40},{28,44},{32,4... | collective-permute-start | bytes 442376 | tf_op jit(solution)/shard_map/ppermute | solution.py:30
  112.4 3.6 %collective-permute-start.7 = (f32[96,384]{1,0:T(8,128)S(1)}, f32[96,384]{1,0:T(8,128)S(1)}, u32[]{:S(2)}, u32[]{:S(2)}) collective-permute-start(f32[96,384]{1,0:T(8,128)S(1)} %get-tuple-element.21), channel_id=1, source_target_pairs={{16,0},{20,4},{24,8},{28,12},{32,16},{36,20},{40,24},{44,28},{48,3... | collective-permute-start | bytes 442376 | tf_op jit(solution)/shard_map/ppermute | solution.py:30
  117.0 2.9 collective-permute-done.7
  120.0 3.3 %scatter_fusion.1 = f32[512,384]{1,0:T(8,128)S(1)} fusion(f32[512,384]{1,0:T(8,128)S(1)} %copy.28, s32[384]{0:T(512)S(1)} %fusion.31, f32[384,384]{1,0:T(8,128)S(1)} %bitcast_multiply_fusion.3), kind=kCustom, calls=%fused_computation.7 | custom fusion | flops 147456 | bytes 1771008 | tf_op jit(solution)/shard_map/scatter-add | solution.py:72
  123.3 4.8 %fusion.5 = f32[512,384]{0,1:T(8,128)} fusion(f32[1,1,512,512]{3,2,1,0:T(8,128)} %param.7, f32[1,1,512,384]{2,3,1,0:T(8,128)S(1)} %copy.24, f32[512,384]{1,0:T(8,128)S(1)} %scatter_fusion.1), kind=kOutput, calls=%fused_computation.21 | convolution fusion | flops 1208352768 | bytes 3407872 | tf_op jit(solution)/shard_map/dot_general | solution.py:34
  132.9 4.8 %collective-permute-start.8 = (f32[96,384]{1,0:T(8,128)S(1)}, f32[96,384]{1,0:T(8,128)S(1)}, u32[]{:S(2)}, u32[]{:S(2)}) collective-permute-start(f32[96,384]{1,0:T(8,128)S(1)} %get-tuple-element.14), channel_id=1, source_target_pairs={{0,4},{4,8},{8,12},{12,16},{16,20},{20,24},{24,28},{28,32},{32,36}... | collective-permute-start | bytes 442376 | tf_op jit(solution)/shard_map/ppermute | solution.py:19
  137.7 4.9 %collective-permute-start.10 = (f32[96,384]{1,0:T(8,128)S(1)}, f32[96,384]{1,0:T(8,128)S(1)}, u32[]{:S(2)}, u32[]{:S(2)}) collective-permute-start(f32[96,384]{1,0:T(8,128)S(1)} %get-tuple-element.15), channel_id=1, source_target_pairs={{0,16},{4,20},{8,24},{12,28},{16,32},{20,36},{24,40},{28,44},{32,4... | collective-permute-start | bytes 442376 | tf_op jit(solution)/shard_map/ppermute | solution.py:30
  144.6 3.8 %collective-permute-start.11 = (f32[96,384]{1,0:T(8,128)S(1)}, f32[96,384]{1,0:T(8,128)S(1)}, u32[]{:S(2)}, u32[]{:S(2)}) collective-permute-start(f32[96,384]{1,0:T(8,128)S(1)} %get-tuple-element.17), channel_id=1, source_target_pairs={{16,0},{20,4},{24,8},{28,12},{32,16},{36,20},{40,24},{44,28},{48,3... | collective-permute-start | bytes 442376 | tf_op jit(solution)/shard_map/ppermute | solution.py:30
  149.1 2.9 collective-permute-done.11
  153.0 3.9 %scatter_fusion.2 = f32[512,384]{1,0:T(8,128)S(1)} fusion(f32[512,384]{1,0:T(8,128)S(1)} %copy.30, s32[384]{0:T(512)S(1)} %fusion.31, f32[384,384]{1,0:T(8,128)} %bitcast_multiply_fusion.2), kind=kCustom, calls=%fused_computation.8 | custom fusion | flops 147456 | bytes 1771008 | tf_op jit(solution)/shard_map/scatter-add | solution.py:72
  156.8 2.5 fusion.10
  161.1 52.3 %reduce-scatter.5.cloned.1.call-done = f32[128,384]{0,1:T(8,128)} async-done(((f32[512,384]{0,1:T(8,128)}), f32[128,384]{0,1:T(8,128)}) %reduce-scatter.5.cloned.1.call-update) | async-done | bytes 196624 | tf_op jit(solution)/shard_map/reduce_scatter | solution.py:87
  215.2 3.6 %fusion.3 = f32[512,384]{0,1:T(8,128)} fusion(f32[384,512]{1,0:T(8,128)S(1)} %fusion.24, f32[1,1,512,512]{3,2,1,0:T(8,128)S(1)} %copy-done, f32[512,384]{1,0:T(8,128)S(1)} %scatter_fusion.2, f32[512]{0:T(512)S(1)} %scatter_custom_fusion), kind=kOutput, calls=%fused_computation.16 | convolution fusion | flops 1208549376 | bytes 3409920 | tf_op jit(solution)/shard_map/dot_general | solution.py:34
  223.6 3.7 %collective-permute-start.12 = (f32[96,384]{1,0:T(8,128)S(1)}, f32[96,384]{1,0:T(8,128)S(1)}, u32[]{:S(2)}, u32[]{:S(2)}) collective-permute-start(f32[96,384]{1,0:T(8,128)S(1)} %get-tuple-element.10), channel_id=1, source_target_pairs={{0,4},{4,8},{8,12},{12,16},{16,20},{20,24},{24,28},{28,32},{32,36}... | collective-permute-start | bytes 442376 | tf_op jit(solution)/shard_map/ppermute | solution.py:19
  227.4 4.3 %collective-permute-start.14 = (f32[96,384]{1,0:T(8,128)S(1)}, f32[96,384]{1,0:T(8,128)S(1)}, u32[]{:S(2)}, u32[]{:S(2)}) collective-permute-start(f32[96,384]{1,0:T(8,128)S(1)} %get-tuple-element.11), channel_id=1, source_target_pairs={{0,16},{4,20},{8,24},{12,28},{16,32},{20,36},{24,40},{28,44},{32,4... | collective-permute-start | bytes 442376 | tf_op jit(solution)/shard_map/ppermute | solution.py:30
  233.6 3.4 %collective-permute-start.15 = (f32[96,384]{1,0:T(8,128)S(1)}, f32[96,384]{1,0:T(8,128)S(1)}, u32[]{:S(2)}, u32[]{:S(2)}) collective-permute-start(f32[96,384]{1,0:T(8,128)S(1)} %get-tuple-element.13), channel_id=1, source_target_pairs={{16,0},{20,4},{24,8},{28,12},{32,16},{36,20},{40,24},{44,28},{48,3... | collective-permute-start | bytes 442376 | tf_op jit(solution)/shard_map/ppermute | solution.py:30
  238.2 2.9 collective-permute-done.15
  242.0 3.7 %scatter_fusion.3 = f32[512,384]{1,0:T(8,128)S(1)} fusion(f32[512,384]{1,0:T(8,128)S(1)} %copy.32, s32[384]{0:T(512)S(1)} %fusion.31, f32[384,384]{1,0:T(8,128)} %bitcast_multiply_fusion.1), kind=kCustom, calls=%fused_computation.9 | custom fusion | flops 147456 | bytes 1771008 | tf_op jit(solution)/shard_map/scatter-add | solution.py:72
  245.7 4.8 %fusion.4 = f32[512,384]{0,1:T(8,128)} fusion(f32[1,1,512,512]{3,2,1,0:T(8,128)} %param.7, f32[1,1,512,384]{2,3,1,0:T(8,128)S(1)} %copy.24, f32[512,384]{1,0:T(8,128)S(1)} %scatter_fusion.3, f32[512,384]{1,0:T(8,128)S(1)} %scatter_fusion.1), kind=kOutput, calls=%fused_computation.18 | convolution fusion | flops 1208745984 | bytes 4194304 | tf_op jit(solution)/shard_map/dot_general | solution.py:34
  255.2 4.8 %collective-permute-start.16 = (f32[96,384]{1,0:T(8,128)S(1)}, f32[96,384]{1,0:T(8,128)S(1)}, u32[]{:S(2)}, u32[]{:S(2)}) collective-permute-start(f32[96,384]{1,0:T(8,128)S(1)} %get-tuple-element.6), channel_id=1, source_target_pairs={{0,4},{4,8},{8,12},{12,16},{16,20},{20,24},{24,28},{28,32},{32,36}... | collective-permute-start | bytes 442376 | tf_op jit(solution)/shard_map/ppermute | solution.py:19
  260.0 5.7 %collective-permute-start.18 = (f32[96,384]{1,0:T(8,128)S(1)}, f32[96,384]{1,0:T(8,128)S(1)}, u32[]{:S(2)}, u32[]{:S(2)}) collective-permute-start(f32[96,384]{1,0:T(8,128)S(1)} %get-tuple-element.7), channel_id=1, source_target_pairs={{0,16},{4,20},{8,24},{12,28},{16,32},{20,36},{24,40},{28,44},{32,4... | collective-permute-start | bytes 442376 | tf_op jit(solution)/shard_map/ppermute | solution.py:30
  267.7 2.6 collective-permute-start.19
  272.2 2.9 collective-permute-done.19
  275.2 3.2 %scatter_fusion.4 = f32[512,384]{1,0:T(8,128)S(1)} fusion(f32[512,384]{1,0:T(8,128)S(1)} %copy.34, s32[384]{0:T(512)S(1)} %fusion.31, f32[384,384]{1,0:T(8,128)S(1)} %bitcast_multiply_fusion), kind=kCustom, calls=%fused_computation.10 | custom fusion | flops 147456 | bytes 1771008 | tf_op jit(solution)/shard_map/scatter-add | solution.py:72
  (77 shorter events, 48.5 us)
Async XLA Ops:
  7.2 90.6 %copy-start = (f32[1,1,512,512]{3,2,1,0:T(8,128)S(1)}, f32[1,1,512,512]{3,2,1,0:T(8,128)}, u32[]{:S(2)}) copy-start(f32[1,1,512,512]{3,2,1,0:T(8,128)} %param.8) | copy-start | bytes 3145732
  7.2 1.3 copy-start.5
  7.2 88.9 %reduce-scatter.3.cloned.1.call-start = ((), (), s32[]{:S(2)}) async-start(), calls=%async_computation.2 | async-start | bytes 983040 | tf_op jit(solution)/shard_map/reduce_scatter | solution.py:87
  11.0 17.0 %collective-permute-start = (f32[96,384]{1,0:T(8,128)}, f32[96,384]{1,0:T(8,128)S(1)}, u32[]{:S(2)}, u32[]{:S(2)}) collective-permute-start(f32[96,384]{1,0:T(8,128)} %get-tuple-element.22), channel_id=1, source_target_pairs={{0,4},{4,8},{8,12},{12,16},{16,20},{20,24},{24,28},{28,32},{32,36}... | collective-permute-start | bytes 442376 | tf_op jit(solution)/shard_map/ppermute | solution.py:19
  14.8 13.2 %collective-permute-start.2 = (f32[96,384]{1,0:T(8,128)S(1)}, f32[96,384]{1,0:T(8,128)S(1)}, u32[]{:S(2)}, u32[]{:S(2)}) collective-permute-start(f32[96,384]{1,0:T(8,128)S(1)} %get-tuple-element.23), channel_id=1, source_target_pairs={{0,16},{4,20},{8,24},{12,28},{16,32},{20,36},{24,40},{28,44},{32,4... | collective-permute-start | bytes 442376 | tf_op jit(solution)/shard_map/ppermute | solution.py:30
  19.3 8.7 %collective-permute-start.1 = (f32[96,384]{1,0:T(8,128)S(1)}, f32[96,384]{1,0:T(8,128)S(1)}, u32[]{:S(2)}, u32[]{:S(2)}) collective-permute-start(f32[96,384]{1,0:T(8,128)S(1)} %get-tuple-element.24), channel_id=1, source_target_pairs={{4,0},{8,4},{12,8},{16,12},{20,16},{24,20},{28,24},{32,28},{36,32}... | collective-permute-start | bytes 442376 | tf_op jit(solution)/shard_map/ppermute | solution.py:22
  21.2 7.5 %collective-permute-start.3 = (f32[96,384]{1,0:T(8,128)S(1)}, f32[96,384]{1,0:T(8,128)}, u32[]{:S(2)}, u32[]{:S(2)}) collective-permute-start(f32[96,384]{1,0:T(8,128)S(1)} %get-tuple-element.25), channel_id=1, source_target_pairs={{16,0},{20,4},{24,8},{28,12},{32,16},{36,20},{40,24},{44,28},{48,3... | collective-permute-start | bytes 442376 | tf_op jit(solution)/shard_map/ppermute | solution.py:30
  29.8 3.2 %copy-start.2 = (f32[1,1,512,128]{3,2,1,0:T(8,128)S(1)}, f32[1,1,512,128]{3,2,1,0:T(8,128)}, u32[]{:S(2)}) copy-start(f32[1,1,512,128]{3,2,1,0:T(8,128)} %param.9) | copy-start | bytes 786436
  33.0 1.5 copy-start.3
  36.2 177.2 %reduce-scatter.5.cloned.1.call-start = ((), (), s32[]{:S(2)}) async-start(), calls=%async_computation.3 | async-start | bytes 983040 | tf_op jit(solution)/shard_map/reduce_scatter | solution.py:87
  102.6 13.5 %collective-permute-start.4 = (f32[96,384]{1,0:T(8,128)S(1)}, f32[96,384]{1,0:T(8,128)S(1)}, u32[]{:S(2)}, u32[]{:S(2)}) collective-permute-start(f32[96,384]{1,0:T(8,128)S(1)} %get-tuple-element.18), channel_id=1, source_target_pairs={{0,4},{4,8},{8,12},{12,16},{16,20},{20,24},{24,28},{28,32},{32,36}... | collective-permute-start | bytes 442376 | tf_op jit(solution)/shard_map/ppermute | solution.py:19
  106.4 9.6 %collective-permute-start.6 = (f32[96,384]{1,0:T(8,128)S(1)}, f32[96,384]{1,0:T(8,128)S(1)}, u32[]{:S(2)}, u32[]{:S(2)}) collective-permute-start(f32[96,384]{1,0:T(8,128)S(1)} %get-tuple-element.19), channel_id=1, source_target_pairs={{0,16},{4,20},{8,24},{12,28},{16,32},{20,36},{24,40},{28,44},{32,4... | collective-permute-start | bytes 442376 | tf_op jit(solution)/shard_map/ppermute | solution.py:30
  110.5 6.5 %collective-permute-start.5 = (f32[96,384]{1,0:T(8,128)S(1)}, f32[96,384]{1,0:T(8,128)S(1)}, u32[]{:S(2)}, u32[]{:S(2)}) collective-permute-start(f32[96,384]{1,0:T(8,128)S(1)} %get-tuple-element.20), channel_id=1, source_target_pairs={{4,0},{8,4},{12,8},{16,12},{20,16},{24,20},{28,24},{32,28},{36,32}... | collective-permute-start | bytes 442376 | tf_op jit(solution)/shard_map/ppermute | solution.py:22
  112.4 7.4 %collective-permute-start.7 = (f32[96,384]{1,0:T(8,128)S(1)}, f32[96,384]{1,0:T(8,128)S(1)}, u32[]{:S(2)}, u32[]{:S(2)}) collective-permute-start(f32[96,384]{1,0:T(8,128)S(1)} %get-tuple-element.21), channel_id=1, source_target_pairs={{16,0},{20,4},{24,8},{28,12},{32,16},{36,20},{40,24},{44,28},{48,3... | collective-permute-start | bytes 442376 | tf_op jit(solution)/shard_map/ppermute | solution.py:30
  132.9 15.4 %collective-permute-start.8 = (f32[96,384]{1,0:T(8,128)S(1)}, f32[96,384]{1,0:T(8,128)S(1)}, u32[]{:S(2)}, u32[]{:S(2)}) collective-permute-start(f32[96,384]{1,0:T(8,128)S(1)} %get-tuple-element.14), channel_id=1, source_target_pairs={{0,4},{4,8},{8,12},{12,16},{16,20},{20,24},{24,28},{28,32},{32,36}... | collective-permute-start | bytes 442376 | tf_op jit(solution)/shard_map/ppermute | solution.py:19
  137.7 10.7 %collective-permute-start.10 = (f32[96,384]{1,0:T(8,128)S(1)}, f32[96,384]{1,0:T(8,128)S(1)}, u32[]{:S(2)}, u32[]{:S(2)}) collective-permute-start(f32[96,384]{1,0:T(8,128)S(1)} %get-tuple-element.15), channel_id=1, source_target_pairs={{0,16},{4,20},{8,24},{12,28},{16,32},{20,36},{24,40},{28,44},{32,4... | collective-permute-start | bytes 442376 | tf_op jit(solution)/shard_map/ppermute | solution.py:30
  142.7 6.5 %collective-permute-start.9 = (f32[96,384]{1,0:T(8,128)S(1)}, f32[96,384]{1,0:T(8,128)S(1)}, u32[]{:S(2)}, u32[]{:S(2)}) collective-permute-start(f32[96,384]{1,0:T(8,128)S(1)} %get-tuple-element.16), channel_id=1, source_target_pairs={{4,0},{8,4},{12,8},{16,12},{20,16},{24,20},{28,24},{32,28},{36,32}... | collective-permute-start | bytes 442376 | tf_op jit(solution)/shard_map/ppermute | solution.py:22
  144.6 7.4 %collective-permute-start.11 = (f32[96,384]{1,0:T(8,128)S(1)}, f32[96,384]{1,0:T(8,128)S(1)}, u32[]{:S(2)}, u32[]{:S(2)}) collective-permute-start(f32[96,384]{1,0:T(8,128)S(1)} %get-tuple-element.17), channel_id=1, source_target_pairs={{16,0},{20,4},{24,8},{28,12},{32,16},{36,20},{40,24},{44,28},{48,3... | collective-permute-start | bytes 442376 | tf_op jit(solution)/shard_map/ppermute | solution.py:30
  156.8 2.5 copy-start.4
  223.6 13.4 %collective-permute-start.12 = (f32[96,384]{1,0:T(8,128)S(1)}, f32[96,384]{1,0:T(8,128)S(1)}, u32[]{:S(2)}, u32[]{:S(2)}) collective-permute-start(f32[96,384]{1,0:T(8,128)S(1)} %get-tuple-element.10), channel_id=1, source_target_pairs={{0,4},{4,8},{8,12},{12,16},{16,20},{20,24},{24,28},{28,32},{32,36}... | collective-permute-start | bytes 442376 | tf_op jit(solution)/shard_map/ppermute | solution.py:19
  227.4 9.6 %collective-permute-start.14 = (f32[96,384]{1,0:T(8,128)S(1)}, f32[96,384]{1,0:T(8,128)S(1)}, u32[]{:S(2)}, u32[]{:S(2)}) collective-permute-start(f32[96,384]{1,0:T(8,128)S(1)} %get-tuple-element.11), channel_id=1, source_target_pairs={{0,16},{4,20},{8,24},{12,28},{16,32},{20,36},{24,40},{28,44},{32,4... | collective-permute-start | bytes 442376 | tf_op jit(solution)/shard_map/ppermute | solution.py:30
  231.7 6.5 %collective-permute-start.13 = (f32[96,384]{1,0:T(8,128)S(1)}, f32[96,384]{1,0:T(8,128)S(1)}, u32[]{:S(2)}, u32[]{:S(2)}) collective-permute-start(f32[96,384]{1,0:T(8,128)S(1)} %get-tuple-element.12), channel_id=1, source_target_pairs={{4,0},{8,4},{12,8},{16,12},{20,16},{24,20},{28,24},{32,28},{36,32}... | collective-permute-start | bytes 442376 | tf_op jit(solution)/shard_map/ppermute | solution.py:22
  233.6 7.4 %collective-permute-start.15 = (f32[96,384]{1,0:T(8,128)S(1)}, f32[96,384]{1,0:T(8,128)S(1)}, u32[]{:S(2)}, u32[]{:S(2)}) collective-permute-start(f32[96,384]{1,0:T(8,128)S(1)} %get-tuple-element.13), channel_id=1, source_target_pairs={{16,0},{20,4},{24,8},{28,12},{32,16},{36,20},{40,24},{44,28},{48,3... | collective-permute-start | bytes 442376 | tf_op jit(solution)/shard_map/ppermute | solution.py:30
  255.2 16.0 %collective-permute-start.16 = (f32[96,384]{1,0:T(8,128)S(1)}, f32[96,384]{1,0:T(8,128)S(1)}, u32[]{:S(2)}, u32[]{:S(2)}) collective-permute-start(f32[96,384]{1,0:T(8,128)S(1)} %get-tuple-element.6), channel_id=1, source_target_pairs={{0,4},{4,8},{8,12},{12,16},{16,20},{20,24},{24,28},{28,32},{32,36}... | collective-permute-start | bytes 442376 | tf_op jit(solution)/shard_map/ppermute | solution.py:19
  260.0 11.2 %collective-permute-start.18 = (f32[96,384]{1,0:T(8,128)S(1)}, f32[96,384]{1,0:T(8,128)S(1)}, u32[]{:S(2)}, u32[]{:S(2)}) collective-permute-start(f32[96,384]{1,0:T(8,128)S(1)} %get-tuple-element.7), channel_id=1, source_target_pairs={{0,16},{4,20},{8,24},{12,28},{16,32},{20,36},{24,40},{28,44},{32,4... | collective-permute-start | bytes 442376 | tf_op jit(solution)/shard_map/ppermute | solution.py:30
  265.7 6.5 %collective-permute-start.17 = (f32[96,384]{1,0:T(8,128)S(1)}, f32[96,384]{1,0:T(8,128)S(1)}, u32[]{:S(2)}, u32[]{:S(2)}) collective-permute-start(f32[96,384]{1,0:T(8,128)S(1)} %get-tuple-element.8), channel_id=1, source_target_pairs={{4,0},{8,4},{12,8},{16,12},{20,16},{24,20},{28,24},{32,28},{36,32}... | collective-permute-start | bytes 442376 | tf_op jit(solution)/shard_map/ppermute | solution.py:22
  267.7 7.4 %collective-permute-start.19 = (f32[96,384]{1,0:T(8,128)S(1)}, f32[96,384]{1,0:T(8,128)S(1)}, u32[]{:S(2)}, u32[]{:S(2)}) collective-permute-start(f32[96,384]{1,0:T(8,128)S(1)} %get-tuple-element.9), channel_id=1, source_target_pairs={{16,0},{20,4},{24,8},{28,12},{32,16},{36,20},{40,24},{44,28},{48,3... | collective-permute-start | bytes 442376 | tf_op jit(solution)/shard_map/ppermute | solution.py:30
  278.4 0.9 copy-start.1
Sparse Core Ops, SparseCore 0:
  36.3 59.6 reduce-scatter.2
  161.2 52.1 reduce-scatter.4
where the time goes:
time: 291 us; the launch traced here: 286 us
  waiting for transfers between devices  128 us (44%)
  starting transfers between devices  70.6 us (24%)
  matrix products  26.8 us (9%)
  local copies, waits for them, and re-layouts  24.5 us (8%)
  other arithmetic  21.6 us (7%)
  between operations  14.6 us (5%)
    reduce_scatter x2, waiting for transfers between devices, local(): lax.psum_scatter(partial_terms, 'grp', scatter_dimension=0, tiled=True)  112 us
    ppermute x10, starting transfers between devices, from_behind(): return lax.ppermute(shard, axis, pairs)  40.1 us
    dot_general x8, matrix products, matmul(): jnp.dot(left, right, precision=highest, preferred_element_type=jnp.float32)  22.8 us
    ppermute x5, starting transfers between devices, padded(): lax.ppermute(lax.slice_in_dim(block, block.shape[dim] - width, None, axis...  20.9 us
    scatter-add x5, other arithmetic, assemble(): return vector_rows.at[flat_rows].add(incoming.reshape(4 * block_width, -1))  17.2 us
    ppermute x10, waiting for transfers between devices, from_behind(): return lax.ppermute(shard, axis, pairs)  12.1 us
    gather x5, local copies, waits for them, and re-layouts, assemble(): picked = vector_rows[flat_rows].reshape(4, block_width, -1)  10.1 us
    ppermute x5, starting transfers between devices, padded(): lax.ppermute(lax.slice_in_dim(block, 0, width, axis=dim), axis, backward)  9.6 us
  transfers between devices with their start and end apart: 22, of which 11 were waited for; matrix products, arithmetic and copies ran while one was open for 2% of the time, Pallas kernels for 0%

commit v1 on v0

v1 whole, which is shorter than its diff:
```python
import functools

import jax
import jax.numpy as jnp
from jax import lax
from jax.experimental import pallas as pl
from jax.experimental.pallas import tpu as pltpu
from jax.sharding import PartitionSpec as P

ITERS = 2
ROW_SUBS = 4
COLS = 128
MESH = pl.DeviceIdType.MESH
F32 = jnp.float32
BF16 = jnp.bfloat16


def split(value):
    high = value.astype(BF16)
    return high, (value - high.astype(F32)).astype(BF16)


def dot(left, right):
    return jnp.dot(left, right, preferred_element_type=F32)


def dot_three(left_high, left_low, right):
    high, low = split(right)
    width = right.shape[1]
    both = dot(left_high, jnp.concatenate([high, low], axis=1))
    return both[:, :width] + both[:, width:] + dot(left_low, high)


def select_rows(chosen, value):
    high, low = split(value)
    width = value.shape[1]
    both = dot(chosen, jnp.concatenate([high, low], axis=1))
    return both[:, :width] + both[:, width:]


def kernel(
    load_ref, schur_ref, solve_ref, modes_ref, cluster_ref, rows_ref,
    x_out, r_out,
    load_v, schur_v, solve_v, modes_v, cluster_v,
    pick, pick_t, schur_h, schur_l, solve_h, solve_l,
    modes_h, modes_l, modes_th, modes_tl, pair_h, pair_l, extra,
    vec, inc, xs, proj, near, own, far_out, far_in, out_x, out_r,
    in_sem, out_sem, a_send, a_recv, n_send, n_recv, f_send, f_recv, e_send, e_recv,
):
    n_sub = lax.axis_size("sub")
    sub = lax.axis_index("sub")
    grp = lax.axis_index("grp")
    rows, loads = load_v.shape
    chunks = loads // COLS
    width = rows_ref.shape[1]
    shared = 4 * width
    rest = rows - shared
    modes = modes_v.shape[1]
    half = COLS // 2
    near_a = grp + 1 - 2 * lax.rem(grp, 2)
    near_b = 3 - grp
    offsets = (-1, 1, -ROW_SUBS, ROW_SUBS)
    targets = [sub + offset for offset in offsets]
    there = [sub > 0, sub < n_sub - 1, sub >= ROW_SUBS, sub < n_sub - ROW_SUBS]

    loads_in = [
        pltpu.make_async_copy(load_ref, load_v, in_sem.at[0]),
        pltpu.make_async_copy(cluster_ref, cluster_v, in_sem.at[1]),
        pltpu.make_async_copy(modes_ref, modes_v, in_sem.at[2]),
        pltpu.make_async_copy(solve_ref, solve_v, in_sem.at[3]),
        pltpu.make_async_copy(schur_ref, schur_v, in_sem.at[4]),
    ]
    for copy in loads_in:
        copy.start()

    barrier = pltpu.get_barrier_semaphore()
    greeted = jnp.int32(2)
    for k in range(4):
        @pl.when(there[k])
        def _():
            pl.semaphore_signal(barrier, 1, device_id=(targets[k], grp), device_id_type=MESH)

        greeted = greeted + there[k].astype(jnp.int32)
    for other in (near_a, near_b):
        pl.semaphore_signal(barrier, 1, device_id=(sub, other), device_id_type=MESH)

    for k in range(4):
        @pl.when(jnp.logical_not(there[k]))
        def _():
            for step in range(2 * ITERS + 1):
                for c in range(chunks):
                    inc[step, c, pl.ds(k * width, width), :] = jnp.zeros((width, COLS), F32)

    def swap(step, c, k):
        rows_at = pl.ds(k * width, width)
        return pltpu.make_async_remote_copy(
            src_ref=vec.at[step, c, rows_at, :],
            dst_ref=inc.at[step, c, pl.ds((k ^ 1) * width, width), :],
            send_sem=a_send.at[step, c, k],
            recv_sem=a_recv.at[step, c, k ^ 1],
            device_id=(targets[k], grp),
            device_id_type=MESH,
        )

    def arrival(step, c, k):
        rows_at = pl.ds(k * width, width)
        return pltpu.make_async_remote_copy(
            src_ref=vec.at[step, c, rows_at, :],
            dst_ref=inc.at[step, c, rows_at, :],
            send_sem=a_send.at[step, c, k],
            recv_sem=a_recv.at[step, c, k],
            device_id=(targets[k], grp),
            device_id_type=MESH,
        )

    def exchange(step, c):
        for k in (2, 3, 0, 1):
            @pl.when(there[k])
            def _():
                swap(step, c, k).start()

    def arrive(step, c):
        for k in (0, 1, 2, 3):
            @pl.when(there[k])
            def _():
                arrival(step, c, k).wait_recv()

    def assembled(step, c):
        return jnp.concatenate(
            [vec[step, c, :shared, :] + inc[step, c], vec[step, c, shared:, :]], axis=0
        )

    def near_copy(it, c, which):
        at = pl.ds(which * half, half)
        return pltpu.make_async_remote_copy(
            src_ref=proj.at[it, c, at, :],
            dst_ref=near.at[it, c, at, :],
            send_sem=n_send.at[it, c, which],
            recv_sem=n_recv.at[it, c, which],
            device_id=(sub, near_b if which else near_a),
            device_id_type=MESH,
        )

    def far_copy(it, c, which):
        at = pl.ds(which * half, half)
        return pltpu.make_async_remote_copy(
            src_ref=far_out.at[it, c, at, :],
            dst_ref=far_in.at[it, c, at, :],
            send_sem=f_send.at[it, c, which],
            recv_sem=f_recv.at[it, c, which],
            device_id=(sub, near_a if which else near_b),
            device_id_type=MESH,
        )

    extra_copy = pltpu.make_async_remote_copy(
        src_ref=cluster_v.at[pl.ds((3 - near_a) * modes, modes), :],
        dst_ref=extra,
        send_sem=e_send,
        recv_sem=e_recv,
        device_id=(sub, near_a),
        device_id_type=MESH,
    )

    eye_i = lax.broadcasted_iota(jnp.int32, (width, width), 0)
    eye_j = lax.broadcasted_iota(jnp.int32, (width, width), 1)
    lane = lax.broadcasted_iota(jnp.int32, (width, rows), 1).astype(F32)
    taken = jnp.zeros((1, rows), F32)
    for k in range(4):
        along = rows_ref[k : k + 1, :].astype(F32)
        column = jnp.sum(jnp.where(eye_i == eye_j, along, 0.0), axis=1, keepdims=True)
        hot = jnp.where(column == lane, 1.0, 0.0)
        taken = taken + jnp.sum(hot, axis=0, keepdims=True)
        pick[k * width : (k + 1) * width, :] = hot.astype(BF16)

    loads_in[0].wait()
    pl.semaphore_wait(barrier, greeted)

    def start(c, carry):
        at = pl.ds(pl.multiple_of(c * COLS, COLS), COLS)
        vec[0, c, :shared, :] = select_rows(pick[:shared, :], load_v[:, at])
        exchange(0, c)
        return carry

    lax.fori_loop(0, chunks, start, 0)
    loads_in[1].wait()
    extra_copy.start()

    free = 1.0 - taken
    order_i = lax.broadcasted_iota(jnp.int32, (rows, rows), 0)
    order_j = lax.broadcasted_iota(jnp.int32, (rows, rows), 1)
    below = jnp.where(order_i < order_j, 1.0, 0.0).astype(BF16)
    rank = dot(jnp.broadcast_to(free, (16, rows)).astype(BF16), below)[:1, :]
    place = lax.broadcasted_iota(jnp.int32, (rest, rows), 0).astype(F32)
    pick[shared:, :] = jnp.where((rank == place) & (free > 0.5), 1.0, 0.0).astype(BF16)
    for c in range(chunks):
        vec[0, c, shared:, :] = select_rows(pick[shared:, :], load_v[:, c * COLS : (c + 1) * COLS])
    for tile in range(rows // 128):
        at = slice(tile * 128, (tile + 1) * 128)
        pick_t[:, at] = jnp.transpose(pick[at, :].astype(F32)).astype(BF16)

    def weights(index):
        total = jnp.ones(index.shape, F32)
        for k in range(4):
            inside = (index >= k * width) & (index < (k + 1) * width)
            total = jnp.where(inside & there[k], 0.5, total)
        return total

    row_weight = weights(lax.broadcasted_iota(jnp.int32, (rows, 1), 0))
    col_weight = weights(lax.broadcasted_iota(jnp.int32, (1, rows), 1))

    loads_in[2].wait()
    basis = row_weight * select_rows(pick[...], modes_v[...])
    modes_h[...], modes_l[...] = split(basis)
    modes_th[...], modes_tl[...] = split(jnp.transpose(basis))

    def reorder(matrix, high_ref, low_ref, scale):
        tile = 128
        for part, into in zip(split(matrix[...]), (high_ref, low_ref)):
            for i in range(rows // tile):
                at = slice(i * tile, (i + 1) * tile)
                moved = dot(pick[at, :], part).astype(BF16)
                moved = dot(moved, pick_t[...])
                if scale is not None:
                    moved = moved * (scale * row_weight[at, :] * col_weight)
                into[at, :] = moved.astype(BF16)

    loads_in[3].wait()
    reorder(solve_v, solve_h, solve_l, 0.5)

    def project(it, c):
        step = 2 * it
        arrive(step, c)
        current = assembled(step, c)
        terms = dot_three(modes_th[...], modes_tl[...], current)
        proj[it, c] = jnp.transpose(terms)
        near_copy(it, c, 0).start()
        near_copy(it, c, 1).start()

    def fine(it, c):
        step = 2 * it
        vec[step + 1, c] = dot_three(solve_h[...], solve_l[...], assembled(step, c))

    def pairs():
        def block(k):
            return 0.5 * cluster_v[pl.ds(pl.multiple_of(k * modes, modes), modes), :]

        to_a, to_b, same = block(near_a), block(near_b), block(grp)
        extra_copy.wait_recv()
        cross = 0.5 * extra[...]
        first = jnp.concatenate(
            [
                jnp.concatenate([jnp.transpose(to_b), same], axis=1),
                jnp.concatenate([jnp.transpose(cross), to_a], axis=1),
            ],
            axis=0,
        )
        second = jnp.concatenate(
            [
                jnp.concatenate([jnp.transpose(to_a), same], axis=1),
                jnp.concatenate([cross, to_b], axis=1),
            ],
            axis=0,
        )
        pair_h[0], pair_l[0] = split(first)
        pair_h[1], pair_l[1] = split(second)

    def combine(it, c):
        for which in range(2):
            at = slice(which * half, (which + 1) * half)
            near_copy(it, c, which).wait_recv()
            known = jnp.concatenate([proj[it, c, at, :], near[it, c, at, :]], axis=1)
            high, low = split(known)
            mixed = (
                dot(high, pair_h[which]) + dot(low, pair_h[which]) + dot(high, pair_l[which])
            )
            far_out[it, c, at, :] = mixed[:, :modes]
            far_copy(it, c, which).start()
            own[c, at, :] = mixed[:, modes:]

    def correct(it, c):
        for which in range(2):
            far_copy(it, c, which).wait_recv()
        coarse = jnp.transpose(own[c] + far_in[it, c])
        step = 2 * it + 1
        vec[step, c] = vec[step, c] + dot_three(modes_h[...], modes_l[...], coarse)
        exchange(step, c)

    def advance(it, c):
        step = 2 * it + 1
        arrive(step, c)
        value = assembled(step, c)
        if it > 0:
            value = value + xs[c]
        xs[c] = value
        vec[step + 1, c] = vec[0, c] - dot_three(schur_h[...], schur_l[...], value)
        exchange(step + 1, c)

    def every(stage, *args):
        def body(c, carry):
            stage(*args, c)
            return carry

        lax.fori_loop(0, chunks, body, 0)

    for it in range(ITERS):
        every(project, it)
        if it == 0:
            pairs()
        every(fine, it)
        every(combine, it)
        if it == 0:
            loads_in[4].wait()
            reorder(schur_v, schur_h, schur_l, None)
        every(correct, it)
        every(advance, it)

    for c in range(chunks):
        at = pl.ds(c * COLS, COLS)
        out_x[:, c * COLS : (c + 1) * COLS] = select_rows(pick_t[...], xs[c])
    write_x = pltpu.make_async_copy(out_x, x_out, out_sem.at[0])
    write_x.start()
    last = 2 * ITERS
    for c in range(chunks):
        arrive(last, c)
        out_r[:, c * COLS : (c + 1) * COLS] = select_rows(pick_t[...], assembled(last, c))
    write_r = pltpu.make_async_copy(out_r, r_out, out_sem.at[1])
    write_r.start()

    extra_copy.wait_send()

    def drain(c, carry):
        for step in range(2 * ITERS + 1):
            for k in range(4):
                @pl.when(there[k])
                def _():
                    swap(step, c, k).wait_send()
        for it in range(ITERS):
            for which in range(2):
                near_copy(it, c, which).wait_send()
                far_copy(it, c, which).wait_send()
        return carry

    lax.fori_loop(0, chunks, drain, 0)
    write_x.wait()
    write_r.wait()


def local(load_terms, schur_matrix, local_inverse, coarse_modes, cluster_inverse, row_blocks):
    rows, loads = load_terms.shape[2:]
    modes = coarse_modes.shape[3]
    width = row_blocks.shape[3]
    chunks = loads // COLS
    steps = 2 * ITERS + 1
    half = COLS // 2
    any_spec = pl.BlockSpec(memory_space=pl.ANY)
    vmem_spec = pl.BlockSpec(memory_space=pltpu.VMEM)
    dma = pltpu.SemaphoreType.DMA
    out = jax.ShapeDtypeStruct((rows, loads), F32)
    solution, residual = pl.pallas_call(
        kernel,
        out_shape=(out, out),
        in_specs=[any_spec] * 5 + [vmem_spec],
        out_specs=(any_spec, any_spec),
        scratch_shapes=[
            pltpu.VMEM((rows, loads), F32),
            pltpu.VMEM((rows, rows), F32),
            pltpu.VMEM((rows, rows), F32),
            pltpu.VMEM((rows, modes), F32),
            pltpu.VMEM(cluster_inverse.shape[1:], F32),
            pltpu.VMEM((rows, rows), BF16),
            pltpu.VMEM((rows, rows), BF16),
            pltpu.VMEM((rows, rows), BF16),
            pltpu.VMEM((rows, rows), BF16),
            pltpu.VMEM((rows, rows), BF16),
            pltpu.VMEM((rows, rows), BF16),
            pltpu.VMEM((rows, modes), BF16),
            pltpu.VMEM((rows, modes), BF16),
            pltpu.VMEM((modes, rows), BF16),
            pltpu.VMEM((modes, rows), BF16),
            pltpu.VMEM((2, 2 * modes, 2 * modes), BF16),
            pltpu.VMEM((2, 2 * modes, 2 * modes), BF16),
            pltpu.VMEM((modes, modes), F32),
            pltpu.VMEM((steps, chunks, rows, COLS), F32),
            pltpu.VMEM((steps, chunks, 4 * width, COLS), F32),
            pltpu.VMEM((chunks, rows, COLS), F32),
            pltpu.VMEM((ITERS, chunks, COLS, modes), F32),
            pltpu.VMEM((ITERS, chunks, COLS, modes), F32),
            pltpu.VMEM((chunks, COLS, modes), F32),
            pltpu.VMEM((ITERS, chunks, COLS, modes), F32),
            pltpu.VMEM((ITERS, chunks, COLS, modes), F32),
            pltpu.VMEM((rows, loads), F32),
            pltpu.VMEM((rows, loads), F32),
            dma((5,)),
            dma((2,)),
            dma((steps, chunks, 4)),
            dma((steps, chunks, 4)),
            dma((ITERS, chunks, 2)),
            dma((ITERS, chunks, 2)),
            dma((ITERS, chunks, 2)),
            dma((ITERS, chunks, 2)),
            dma,
            dma,
        ],
        compiler_params=pltpu.CompilerParams(
            collective_id=0, has_side_effects=True, vmem_limit_bytes=60 * 1024 * 1024
        ),
    )(
        load_terms[0, 0], schur_matrix[0, 0], local_inverse[0, 0], coarse_modes[0, 0],
        cluster_inverse[0], row_blocks[0, 0],
    )
    return solution[None, None], residual[None, None]


def solution(mesh):
    return jax.shard_map(
        local,
        mesh=mesh,
        in_specs=(
            P("sub", "grp", None, None),
            P("sub", "grp", None, None),
            P("sub", "grp", None, None),
            P("sub", "grp", None, None),
            P("sub", None, "grp"),
            P("sub", "grp", None, None),
        ),
        out_specs=(P("sub", "grp", None, None), P("sub", "grp", None, None)),
        check_vma=False,
    )
```

time: 291 us -> 102 us (0.35)
  the two profiles are of different devices: /device:TPU:7 before, /device:TPU:40 now
where the time goes in v1:
time: 102 us
  Pallas kernels  98.4 us (96%)
  local copies, waits for them, and re-layouts  3.02 us (3%)
    pallas_call x1, Pallas kernels, local(): pl.pallas_call(kernel, out_shape=(out, out), in_specs=[any_spec] * 5 + [v...  98.4 us
    unnamed x4, local copies, waits for them, and re-layouts  3.02 us

profile of v1, /device:TPU:40, one launch (start us, length us, event | category | flops | bytes accessed | tf_op | source)
XLA Modules:
  0.0 102.1 jit_solution(3346652176947578221)
XLA Ops:
  0.6 98.4 %shard_map.77 = (f32[512,384]{1,0:T(8,128)}, f32[512,384]{1,0:T(8,128)}) custom-call(f32[512,384]{1,0:T(8,128)} %bitcast.12, f32[512,512]{1,0:T(8,128)} %bitcast.8, f32[512,512]{1,0:T(8,128)} %bitcast.9, f32[512,128]{1,0:T(8,128)} %bitcast.13, f32[512,128]{1,0:T(8,128)} %bitcast.14, s32[4,96]{1,0:T(4,128)} %bitcast.15), custom_call_target="tpu_custom_call" | custom-call | tf_op jit(solution)/shard_map/pallas_call | solution.py:359
  99.0 0.0 copy-start
  99.1 2.1 %copy.10 = f32[1,1,512,384]{3,2,1,0:T(8,128)} copy(f32[1,1,512,384]{3,2,1,0:T(8,128)} %bitcast.11) | data formatting | bytes 1572864
  101.2 0.0 copy-done
  101.2 0.9 copy.11
Async XLA Ops:
  99.0 2.1 %copy-start = (f32[512,384]{1,0:T(8,128)S(1)}, f32[512,384]{1,0:T(8,128)}, u32[]{:S(2)}) copy-start(f32[512,384]{1,0:T(8,128)} %get-tuple-element.5) | copy-start | bytes 2359300

commit v2 on v1

v2 whole, which is shorter than its diff:
```python
import functools

import jax
import jax.numpy as jnp
from jax import lax
from jax.experimental import pallas as pl
from jax.experimental.pallas import tpu as pltpu
from jax.sharding import PartitionSpec as P

ITERS = 2
ROW_SUBS = 4
COLS = 128
HALF = 64
MESH = pl.DeviceIdType.MESH
F32 = jnp.float32
BF16 = jnp.bfloat16


def split(value):
    high = value.astype(BF16)
    return high, (value - high.astype(F32)).astype(BF16)


def dot(left, right):
    return jnp.dot(left, right, preferred_element_type=F32)


def select_rows(chosen, value):
    high, low = split(value)
    width = value.shape[1]
    both = dot(chosen, jnp.concatenate([high, low], axis=1))
    return both[:, :width] + both[:, width:]


def left_lanes(shape):
    return lax.broadcasted_iota(jnp.int32, shape, 1) < HALF


def turn(value):
    return pltpu.roll(value, HALF, 1)


def parts(packed):
    left = left_lanes(packed.shape)
    high = packed.astype(BF16).astype(F32)
    low = packed - high
    top = jnp.where(left, high, turn(low))
    bottom = jnp.where(left, turn(high), low)
    return jnp.concatenate([top, bottom], axis=0).astype(BF16)


def fold(product):
    middle = product.shape[0] // 2
    top, bottom = product[:middle], product[middle:]
    left = left_lanes(top.shape)
    return jnp.where(left, top + turn(top), bottom + turn(bottom))


def twice(value):
    return jnp.concatenate([value, value], axis=0)


def kernel(
    load_ref, schur_ref, solve_ref, modes_ref, cluster_ref, rows_ref,
    both_out,
    load_v, schur_v, solve_v, modes_v, cluster_v,
    pick, pick_t, schur_hl, solve_hl, modes_hl, modes_thl, pair_h, pair_l, extra,
    vec, inc, xs, rhs, proj, near, own, far_out, far_in, out_x, out_r,
    in_sem, out_sem, a_send, a_recv, n_send, n_recv, f_send, f_recv, e_send, e_recv,
):
    n_sub = lax.axis_size("sub")
    sub = lax.axis_index("sub")
    grp = lax.axis_index("grp")
    rows, loads = load_v.shape
    blocks = loads // COLS
    chunks = 2 * blocks
    width = rows_ref.shape[1]
    piece = width // 2
    middle = rows // 2
    shared = 4 * piece
    modes = modes_v.shape[1]
    share = HALF // 2
    steps = 2 * ITERS + 1
    near_a = grp + 1 - 2 * lax.rem(grp, 2)
    near_b = 3 - grp
    offsets = (-1, 1, -ROW_SUBS, ROW_SUBS)
    targets = [sub + offset for offset in offsets]
    there = [sub > 0, sub < n_sub - 1, sub >= ROW_SUBS, sub < n_sub - ROW_SUBS]

    loads_in = [
        pltpu.make_async_copy(load_ref, load_v, in_sem.at[0]),
        pltpu.make_async_copy(cluster_ref, cluster_v, in_sem.at[1]),
        pltpu.make_async_copy(modes_ref, modes_v, in_sem.at[2]),
        pltpu.make_async_copy(solve_ref, solve_v, in_sem.at[3]),
        pltpu.make_async_copy(schur_ref, schur_v, in_sem.at[4]),
    ]
    for copy in loads_in:
        copy.start()

    barrier = pltpu.get_barrier_semaphore()
    greeted = jnp.int32(2)
    for k in range(4):
        @pl.when(there[k])
        def _():
            pl.semaphore_signal(barrier, 1, device_id=(targets[k], grp), device_id_type=MESH)

        greeted = greeted + there[k].astype(jnp.int32)
    for other in (near_a, near_b):
        pl.semaphore_signal(barrier, 1, device_id=(sub, other), device_id_type=MESH)

    for k in range(4):
        @pl.when(jnp.logical_not(there[k]))
        def _():
            def clear(c, carry):
                for step in range(steps):
                    inc[step, c, pl.ds(k * piece, piece), :] = jnp.zeros((piece, COLS), F32)
                return carry

            lax.fori_loop(0, chunks, clear, 0)

    def swap(step, c, k):
        return pltpu.make_async_remote_copy(
            src_ref=vec.at[step, c, pl.ds(k * piece, piece), :],
            dst_ref=inc.at[step, c, pl.ds((k ^ 1) * piece, piece), :],
            send_sem=a_send.at[c, k],
            recv_sem=a_recv.at[step, c, k ^ 1],
            device_id=(targets[k], grp),
            device_id_type=MESH,
        )

    def arrival(step, c, k):
        rows_at = pl.ds(k * piece, piece)
        return pltpu.make_async_remote_copy(
            src_ref=vec.at[step, c, rows_at, :],
            dst_ref=inc.at[step, c, rows_at, :],
            send_sem=a_send.at[c, k],
            recv_sem=a_recv.at[step, c, k],
            device_id=(targets[k], grp),
            device_id_type=MESH,
        )

    def exchange(step, c):
        for k in (2, 3, 0, 1):
            @pl.when(there[k])
            def _():
                if step > 0:
                    swap(step - 1, c, k).wait_send()
                swap(step, c, k).start()

    def arrive(step, c):
        for k in (0, 1, 2, 3):
            @pl.when(there[k])
            def _():
                arrival(step, c, k).wait_recv()

    def assembled(step, c):
        return jnp.concatenate(
            [vec[step, c, :shared, :] + inc[step, c], vec[step, c, shared:, :]], axis=0
        )

    def near_copy(it, c, which):
        at = pl.ds(which * share, share)
        return pltpu.make_async_remote_copy(
            src_ref=proj.at[it, c, at, :],
            dst_ref=near.at[it, c, at, :],
            send_sem=n_send.at[c, which],
            recv_sem=n_recv.at[it, c, which],
            device_id=(sub, near_b if which else near_a),
            device_id_type=MESH,
        )

    def far_copy(it, c, which):
        at = pl.ds(which * share, share)
        return pltpu.make_async_remote_copy(
            src_ref=far_out.at[it, c, at, :],
            dst_ref=far_in.at[it, c, at, :],
            send_sem=f_send.at[c, which],
            recv_sem=f_recv.at[it, c, which],
            device_id=(sub, near_a if which else near_b),
            device_id_type=MESH,
        )

    extra_copy = pltpu.make_async_remote_copy(
        src_ref=cluster_v.at[pl.ds((3 - near_a) * modes, modes), :],
        dst_ref=extra,
        send_sem=e_send,
        recv_sem=e_recv,
        device_id=(sub, near_a),
        device_id_type=MESH,
    )

    eye_i = lax.broadcasted_iota(jnp.int32, (width, width), 0)
    eye_j = lax.broadcasted_iota(jnp.int32, (width, width), 1)
    lane = lax.broadcasted_iota(jnp.int32, (width, rows), 1).astype(F32)
    taken = jnp.zeros((1, rows), F32)
    for k in range(4):
        along = rows_ref[k : k + 1, :].astype(F32)
        column = jnp.sum(jnp.where(eye_i == eye_j, along, 0.0), axis=1, keepdims=True)
        hot = jnp.where(column == lane, 1.0, 0.0)
        taken = taken + jnp.sum(hot, axis=0, keepdims=True)
        hot = hot.astype(BF16)
        pick[k * piece : (k + 1) * piece, :] = hot[:piece]
        pick[middle + k * piece : middle + (k + 1) * piece, :] = hot[piece:]

    loads_in[0].wait()
    pl.semaphore_wait(barrier, greeted)

    def pack_pair(top, bottom, step, j, at):
        left = left_lanes(top.shape)
        vec[step, 2 * j, at, :] = jnp.where(left, top, turn(bottom))
        vec[step, 2 * j + 1, at, :] = jnp.where(left, turn(top), bottom)

    def start(j, carry):
        at = pl.ds(pl.multiple_of(j * COLS, COLS), COLS)
        chosen = jnp.concatenate([pick[:shared, :], pick[middle : middle + shared, :]], axis=0)
        moved = select_rows(chosen, load_v[:, at])
        pack_pair(moved[:shared], moved[shared:], 0, j, pl.ds(0, shared))
        exchange(0, 2 * j)
        exchange(0, 2 * j + 1)
        return carry

    lax.fori_loop(0, blocks, start, 0)
    loads_in[1].wait()
    extra_copy.start()

    spare = middle - shared
    free = 1.0 - taken
    order_i = lax.broadcasted_iota(jnp.int32, (rows, rows), 0)
    order_j = lax.broadcasted_iota(jnp.int32, (rows, rows), 1)
    below = jnp.where(order_i < order_j, 1.0, 0.0).astype(BF16)
    rank = dot(jnp.broadcast_to(free, (16, rows)).astype(BF16), below)[:1, :]
    place = lax.broadcasted_iota(jnp.int32, (2 * spare, rows), 0).astype(F32)
    others = jnp.where((rank == place) & (free > 0.5), 1.0, 0.0).astype(BF16)
    pick[shared:middle, :] = others[:spare]
    pick[middle + shared :, :] = others[spare:]
    for j in range(blocks):
        moved = select_rows(others, load_v[:, j * COLS : (j + 1) * COLS])
        pack_pair(moved[:spare], moved[spare:], 0, j, pl.ds(shared, spare))

    def weights(index):
        within = lax.rem(index, middle)
        total = jnp.ones(index.shape, F32)
        for k in range(4):
            inside = (within >= k * piece) & (within < (k + 1) * piece)
            total = jnp.where(inside & there[k], 0.5, total)
        return total

    row_weight = weights(lax.broadcasted_iota(jnp.int32, (rows, 1), 0))
    col_weight = weights(lax.broadcasted_iota(jnp.int32, (1, rows), 1))

    loads_in[2].wait()
    basis = row_weight * select_rows(pick[...], modes_v[...])
    high, low = split(basis)
    modes_hl[:, :modes] = high
    modes_hl[:, modes:] = low
    high, low = split(jnp.transpose(basis))
    modes_thl[:, :rows] = high
    modes_thl[:, rows:] = low

    def reorder(matrix, into, scale):
        tile = 128
        for p, part in enumerate(split(matrix[...])):
            for i in range(rows // tile):
                at = slice(i * tile, (i + 1) * tile)
                moved = dot(pick[at, :], part).astype(BF16)
                moved = dot(moved, pick_t[...])
                if scale is not None:
                    moved = moved * (scale * row_weight[at, :] * col_weight)
                into[at, p * rows : (p + 1) * rows] = moved.astype(BF16)

    def project(it, c):
        step = 2 * it
        arrive(step, c)
        sides = parts(assembled(step, c))
        rhs[c] = sides
        terms = jnp.transpose(dot(modes_thl[...], twice(sides)))
        if it > 0:
            for which in range(2):
                near_copy(it - 1, c, which).wait_send()
        proj[it, c] = terms[:HALF] + terms[HALF:]
        near_copy(it, c, 0).start()
        near_copy(it, c, 1).start()

    def fine(it, j):
        step = 2 * it + 1
        sides = jnp.concatenate([rhs[2 * j], rhs[2 * j + 1]], axis=1)
        both = dot(solve_hl[...], twice(sides))
        vec[step, 2 * j] = fold(both[:, :COLS])
        vec[step, 2 * j + 1] = fold(both[:, COLS:])

    def pairs():
        def block(k):
            return 0.5 * cluster_v[pl.ds(pl.multiple_of(k * modes, modes), modes), :]

        to_a, to_b, same = block(near_a), block(near_b), block(grp)
        extra_copy.wait_recv()
        cross = 0.5 * extra[...]
        first = jnp.concatenate(
            [
                jnp.concatenate([jnp.transpose(to_b), same], axis=1),
                jnp.concatenate([jnp.transpose(cross), to_a], axis=1),
            ],
            axis=0,
        )
        second = jnp.concatenate(
            [
                jnp.concatenate([jnp.transpose(to_a), same], axis=1),
                jnp.concatenate([cross, to_b], axis=1),
            ],
            axis=0,
        )
        pair_h[0], pair_l[0] = split(first)
        pair_h[1], pair_l[1] = split(second)

    def combine(it, c):
        for which in range(2):
            at = slice(which * share, (which + 1) * share)
            near_copy(it, c, which).wait_recv()
            known = jnp.concatenate([proj[it, c, at, :], near[it, c, at, :]], axis=1)
            high, low = split(known)
            mixed = dot(jnp.concatenate([high, low], axis=0), pair_h[which])
            mixed = mixed[:share] + mixed[share:] + dot(high, pair_l[which])
            if it > 0:
                far_copy(it - 1, c, which).wait_send()
            far_out[it, c, at, :] = mixed[:, :modes]
            far_copy(it, c, which).start()
            own[c, at, :] = mixed[:, modes:]

    def correct(it, c):
        for which in range(2):
            far_copy(it, c, which).wait_recv()
        coarse = own[c] + far_in[it, c]
        high = coarse.astype(BF16).astype(F32)
        sides = jnp.transpose(jnp.concatenate([high, coarse - high], axis=0)).astype(BF16)
        step = 2 * it + 1
        vec[step, c] = vec[step, c] + fold(dot(modes_hl[...], twice(sides)))
        exchange(step, c)

    def advance(it, c):
        step = 2 * it + 1
        arrive(step, c)
        value = assembled(step, c)
        if it > 0:
            value = value + xs[c]
        xs[c] = value
        vec[step + 1, c] = vec[0, c] - fold(dot(schur_hl[...], twice(parts(value))))
        exchange(step + 1, c)

    def every(stage, it, count):
        def body(c, carry):
            stage(it, c)
            return carry

        lax.fori_loop(0, count, body, 0)

    for it in range(ITERS):
        every(project, it, chunks)
        if it == 0:
            for tile in range(rows // 128):
                at = slice(tile * 128, (tile + 1) * 128)
                pick_t[:, at] = jnp.transpose(pick[at, :].astype(F32)).astype(BF16)
            pairs()
            loads_in[3].wait()
            reorder(solve_v, solve_hl, 0.5)
        if it > 0:
            every(fine, it, blocks)
        every(combine, it, chunks)
        if it == 0:
            every(fine, it, blocks)
            loads_in[4].wait()
            reorder(schur_v, schur_hl, None)
        every(correct, it, chunks)
        every(advance, it, chunks)

    def unpacked(first, second):
        left = left_lanes(first.shape)
        return jnp.concatenate(
            [jnp.where(left, first, turn(second)), jnp.where(left, turn(first), second)], axis=0
        )

    for j in range(blocks):
        at = slice(j * COLS, (j + 1) * COLS)
        out_x[:, at] = 0.5 * select_rows(pick_t[...], unpacked(xs[2 * j], xs[2 * j + 1]))
    write_x = pltpu.make_async_copy(out_x, both_out.at[0], out_sem.at[0])
    write_x.start()
    last = 2 * ITERS
    writes = []
    for j in range(blocks):
        at = slice(j * COLS, (j + 1) * COLS)
        arrive(last, 2 * j)
        arrive(last, 2 * j + 1)
        value = unpacked(assembled(last, 2 * j), assembled(last, 2 * j + 1))
        out_r[j] = 0.5 * select_rows(pick_t[...], value)
        write = pltpu.make_async_copy(
            out_r.at[j], both_out.at[1, :, pl.ds(j * COLS, COLS)], out_sem.at[1 + j]
        )
        write.start()
        writes.append(write)

    extra_copy.wait_send()

    def drain(c, carry):
        for k in range(4):
            @pl.when(there[k])
            def _():
                swap(last, c, k).wait_send()
        for which in range(2):
            near_copy(ITERS - 1, c, which).wait_send()
            far_copy(ITERS - 1, c, which).wait_send()
        return carry

    lax.fori_loop(0, chunks, drain, 0)
    write_x.wait()
    for write in writes:
        write.wait()


def local(load_terms, schur_matrix, local_inverse, coarse_modes, cluster_inverse, row_blocks):
    rows, loads = load_terms.shape[2:]
    modes = coarse_modes.shape[3]
    width = row_blocks.shape[3]
    blocks = loads // COLS
    chunks = 2 * blocks
    steps = 2 * ITERS + 1
    any_spec = pl.BlockSpec(memory_space=pl.ANY)
    vmem_spec = pl.BlockSpec(memory_space=pltpu.VMEM)
    dma = pltpu.SemaphoreType.DMA
    halves = pl.pallas_call(
        kernel,
        out_shape=jax.ShapeDtypeStruct((2, rows, loads), F32),
        in_specs=[any_spec] * 5 + [vmem_spec],
        out_specs=any_spec,
        scratch_shapes=[
            pltpu.VMEM((rows, loads), F32),
            pltpu.VMEM((rows, rows), F32),
            pltpu.VMEM((rows, rows), F32),
            pltpu.VMEM((rows, modes), F32),
            pltpu.VMEM(cluster_inverse.shape[1:], F32),
            pltpu.VMEM((rows, rows), BF16),
            pltpu.VMEM((rows, rows), BF16),
            pltpu.VMEM((rows, 2 * rows), BF16),
            pltpu.VMEM((rows, 2 * rows), BF16),
            pltpu.VMEM((rows, 2 * modes), BF16),
            pltpu.VMEM((modes, 2 * rows), BF16),
            pltpu.VMEM((2, 2 * modes, 2 * modes), BF16),
            pltpu.VMEM((2, 2 * modes, 2 * modes), BF16),
            pltpu.VMEM((modes, modes), F32),
            pltpu.VMEM((steps, chunks, rows // 2, COLS), F32),
            pltpu.VMEM((steps, chunks, 2 * width, COLS), F32),
            pltpu.VMEM((chunks, rows // 2, COLS), F32),
            pltpu.VMEM((chunks, rows, COLS), BF16),
            pltpu.VMEM((ITERS, chunks, HALF, modes), F32),
            pltpu.VMEM((ITERS, chunks, HALF, modes), F32),
            pltpu.VMEM((chunks, HALF, modes), F32),
            pltpu.VMEM((ITERS, chunks, HALF, modes), F32),
            pltpu.VMEM((ITERS, chunks, HALF, modes), F32),
            pltpu.VMEM((rows, loads), F32),
            pltpu.VMEM((blocks, rows, COLS), F32),
            dma((5,)),
            dma((1 + blocks,)),
            dma((chunks, 4)),
            dma((steps, chunks, 4)),
            dma((chunks, 2)),
            dma((ITERS, chunks, 2)),
            dma((chunks, 2)),
            dma((ITERS, chunks, 2)),
            dma,
            dma,
        ],
        compiler_params=pltpu.CompilerParams(
            collective_id=0, has_side_effects=True, vmem_limit_bytes=60 * 1024 * 1024
        ),
    )(
        load_terms[0, 0], schur_matrix[0, 0], local_inverse[0, 0], coarse_modes[0, 0],
        cluster_inverse[0], row_blocks[0, 0],
    )
    return 2.0 * halves[0][None, None], 2.0 * halves[1][None, None]


def solution(mesh):
    return jax.shard_map(
        local,
        mesh=mesh,
        in_specs=(
            P("sub", "grp", None, None),
            P("sub", "grp", None, None),
            P("sub", "grp", None, None),
            P("sub", "grp", None, None),
            P("sub", None, "grp"),
            P("sub", "grp", None, None),
        ),
        out_specs=(P("sub", "grp", None, None), P("sub", "grp", None, None)),
        check_vma=False,
    )
```

time: 102 us -> 99.3 us (0.974)
  the two profiles are of different devices: /device:TPU:40 before, /device:TPU:44 now
where the time goes in v2:
time: 99.3 us; the launch traced here: 99.2 us
  Pallas kernels  95.9 us (97%)
  other arithmetic  2.61 us (3%)
    pallas_call x1, Pallas kernels, local(): pl.pallas_call(kernel, out_shape=jax.ShapeDtypeStruct((2, rows, loads), F...  95.9 us
    mul x1, other arithmetic, local(): return (2.0 * halves[0][None, None], 2.0 * halves[1][None, None])  2.61 us

profile of v2, /device:TPU:44, one launch (start us, length us, event | category | flops | bytes accessed | tf_op | source)
XLA Modules:
  0.0 99.2 jit_solution(13445127198741857927)
XLA Ops:
  0.6 95.9 %shard_map.77 = f32[2,512,384]{2,1,0:T(8,128)} custom-call(f32[512,384]{1,0:T(8,128)} %bitcast.12, f32[512,512]{1,0:T(8,128)} %bitcast.10, f32[512,512]{1,0:T(8,128)} %bitcast.11, f32[512,128]{1,0:T(8,128)} %bitcast.13, f32[512,128]{1,0:T(8,128)} %bitcast.14, s32[4,96]{1,0:T(4,128)} %bitcast.15), custom_call_target="tpu_custom_call" | custom-call | tf_op jit(solution)/shard_map/pallas_call | solution.py:428
  96.6 2.6 %multiply_bitcast_fusion = (f32[1,1,512,384]{3,2,1,0:T(8,128)}, f32[1,1,512,384]{3,2,1,0:T(8,128)}) fusion(f32[2,512,384]{2,1,0:T(8,128)} %shard_map.77), kind=kLoop, calls=%fused_computation | loop fusion | flops 393216 | bytes 3145728 | tf_op jit(solution)/shard_map/mul | solution.py:477

commit v3 on v2

--- a/solution.py
+++ b/solution.py
@@ -64,7 +64,7 @@
     load_ref, schur_ref, solve_ref, modes_ref, cluster_ref, rows_ref,
     both_out,
     load_v, schur_v, solve_v, modes_v, cluster_v,
-    pick, pick_t, schur_hl, solve_hl, modes_hl, modes_thl, pair_h, pair_l, extra,
+    pick, pick_t, schur_hl, solve_hl, modes_hl, modes_thl, pair_h, pair_l, extra, extra_out,
     vec, inc, xs, rhs, proj, near, own, far_out, far_in, out_x, out_r,
     in_sem, out_sem, a_send, a_recv, n_send, n_recv, f_send, f_recv, e_send, e_recv,
 ):
@@ -180,14 +180,17 @@
             device_id_type=MESH,
         )
 
-    extra_copy = pltpu.make_async_remote_copy(
-        src_ref=cluster_v.at[pl.ds((3 - near_a) * modes, modes), :],
-        dst_ref=extra,
-        send_sem=e_send,
-        recv_sem=e_recv,
-        device_id=(sub, near_a),
-        device_id_type=MESH,
-    )
+    quarter = modes // 2
+
+    def extra_copy(which):
+        return pltpu.make_async_remote_copy(
+            src_ref=extra_out.at[which],
+            dst_ref=extra.at[pl.ds(which * quarter, quarter), :],
+            send_sem=e_send.at[which],
+            recv_sem=e_recv.at[which],
+            device_id=(sub, near_b if which else near_a),
+            device_id_type=MESH,
+        )
 
     eye_i = lax.broadcasted_iota(jnp.int32, (width, width), 0)
     eye_j = lax.broadcasted_iota(jnp.int32, (width, width), 1)
@@ -203,7 +206,6 @@
         pick[middle + k * piece : middle + (k + 1) * piece, :] = hot[piece:]
 
     loads_in[0].wait()
-    pl.semaphore_wait(barrier, greeted)
 
     def pack_pair(top, bottom, step, j, at):
         left = left_lanes(top.shape)
@@ -215,13 +217,24 @@
         chosen = jnp.concatenate([pick[:shared, :], pick[middle : middle + shared, :]], axis=0)
         moved = select_rows(chosen, load_v[:, at])
         pack_pair(moved[:shared], moved[shared:], 0, j, pl.ds(0, shared))
-        exchange(0, 2 * j)
-        exchange(0, 2 * j + 1)
         return carry
 
+    def send_first(c, carry):
+        exchange(0, c)
+        return carry
+
     lax.fori_loop(0, blocks, start, 0)
+    pl.semaphore_wait(barrier, greeted)
+    lax.fori_loop(0, chunks, send_first, 0)
     loads_in[1].wait()
-    extra_copy.start()
+    extra_out[0] = cluster_v[pl.ds(pl.multiple_of((3 - near_a) * modes, modes), quarter), :]
+    near_b_near_a = near_b + 1 - 2 * lax.rem(near_b, 2)
+    turned = jnp.transpose(
+        cluster_v[pl.ds(pl.multiple_of(near_b_near_a * modes, modes), modes), :]
+    )
+    extra_out[1] = turned[quarter:]
+    extra_copy(0).start()
+    extra_copy(1).start()
 
     spare = middle - shared
     free = 1.0 - taken
@@ -293,7 +306,8 @@
             return 0.5 * cluster_v[pl.ds(pl.multiple_of(k * modes, modes), modes), :]
 
         to_a, to_b, same = block(near_a), block(near_b), block(grp)
-        extra_copy.wait_recv()
+        extra_copy(0).wait_recv()
+        extra_copy(1).wait_recv()
         cross = 0.5 * extra[...]
         first = jnp.concatenate(
             [
@@ -397,7 +411,8 @@
         write.start()
         writes.append(write)
 
-    extra_copy.wait_send()
+    extra_copy(0).wait_send()
+    extra_copy(1).wait_send()
 
     def drain(c, carry):
         for k in range(4):
@@ -445,6 +460,7 @@
             pltpu.VMEM((2, 2 * modes, 2 * modes), BF16),
             pltpu.VMEM((2, 2 * modes, 2 * modes), BF16),
             pltpu.VMEM((modes, modes), F32),
+            pltpu.VMEM((2, modes // 2, modes), F32),
             pltpu.VMEM((steps, chunks, rows // 2, COLS), F32),
             pltpu.VMEM((steps, chunks, 2 * width, COLS), F32),
             pltpu.VMEM((chunks, rows // 2, COLS), F32),
@@ -464,8 +480,8 @@
             dma((ITERS, chunks, 2)),
             dma((chunks, 2)),
             dma((ITERS, chunks, 2)),
-            dma,
-            dma,
+            dma((2,)),
+            dma((2,)),
         ],
         compiler_params=pltpu.CompilerParams(
             collective_id=0, has_side_effects=True, vmem_limit_bytes=60 * 1024 * 1024

time: 99.3 us -> 97 us (0.977)
  the two profiles are of different devices: /device:TPU:44 before, /device:TPU:7 now
where the time goes in v3:
time: 97 us; the launch traced here: 96.8 us
  Pallas kernels  93.5 us (96%)
  other arithmetic  2.61 us (3%)
    pallas_call x1, Pallas kernels, local(): pl.pallas_call(kernel, out_shape=jax.ShapeDtypeStruct((2, rows, loads), F...  93.5 us
    mul x1, other arithmetic, local(): return (2.0 * halves[0][None, None], 2.0 * halves[1][None, None])  2.61 us

profile of v3, /device:TPU:7, one launch (start us, length us, event | category | flops | bytes accessed | tf_op | source)
XLA Modules:
  0.0 96.8 jit_solution(13419938497693133406)
XLA Ops:
  0.6 93.5 %shard_map.77 = f32[2,512,384]{2,1,0:T(8,128)} custom-call(f32[512,384]{1,0:T(8,128)} %bitcast.12, f32[512,512]{1,0:T(8,128)} %bitcast.10, f32[512,512]{1,0:T(8,128)} %bitcast.11, f32[512,128]{1,0:T(8,128)} %bitcast.13, f32[512,128]{1,0:T(8,128)} %bitcast.14, s32[4,96]{1,0:T(4,128)} %bitcast.15), custom_call_target="tpu_custom_call" | custom-call | tf_op jit(solution)/shard_map/pallas_call | solution.py:443
  94.2 2.6 %multiply_bitcast_fusion = (f32[1,1,512,384]{3,2,1,0:T(8,128)}, f32[1,1,512,384]{3,2,1,0:T(8,128)}) fusion(f32[2,512,384]{2,1,0:T(8,128)} %shard_map.77), kind=kLoop, calls=%fused_computation | loop fusion | flops 393216 | bytes 3145728 | tf_op jit(solution)/shard_map/mul | solution.py:493
